TPU v7x, 128 devices: a whole 4x4x4 slice. The times are simulated.
128 devices in a mesh: row: 16 (over y, z), col: 8 (over x, core).
Axes of the slice: x: 4, y: 4, z: 4, core: 2. Of those that a mesh axis runs over, the one named last changes fastest.
Arguments:
- block_cols: int32 [64, 16], replicated, may hold values from -1 to 63, as said below
- step_dir: bfloat16 [64, 16, 128, 128], P('row', 'col')
- intersection: bfloat16 [64, 16, 128, 128], P('row', 'col')
- density: bfloat16 [64, 16, 128, 128], P('row', 'col')
- kohn_sham: bfloat16 [64, 16, 128, 128], P('row', 'col')
Outputs:
- commutator: bfloat16 [64, 16, 128, 128], P('row', 'col')
- trace_value: float32 [], replicated
Inputs may be any that keep to these rules, and one draw needn't show every extreme that they name: block_cols[i, s] is -1 or a block column of group s // 2, that is from (s // 2) * 8 to (s // 2 + 1) * 8 - 1; the live entries of one block row within one group are distinct; the pattern is symmetric (j is live in row i exactly when i is live in row j) and holds every diagonal block.
All inputs are finite; a program needn't handle non-finite values.
Results may differ from a plain program's by a relative error of at most 0.0057.
Values may be sent and summed in bfloat16 or wider, within the bound.
A program may use at most 64 MiB of HBM per device.

v0:
```python
import jax
import jax.numpy as jnp
from jax import lax
from jax.sharding import PartitionSpec as P


def per_device(block_cols, step_dir, intersection, density, kohn_sham):
    row_total = step_dir.shape[0]
    slot_total = step_dir.shape[1]
    block_size = step_dir.shape[2]
    col_groups = lax.axis_size("col")
    blocks_total = block_cols.shape[0]
    row_index = lax.axis_index("row")
    col_index = lax.axis_index("col")
    own_rows = lax.dynamic_slice_in_dim(block_cols, row_index * row_total, row_total, 0)
    own_cols = lax.dynamic_slice_in_dim(own_rows, col_index * slot_total, slot_total, 1)
    group_cols = lax.dynamic_slice_in_dim(block_cols, col_index * slot_total, slot_total, 1)
    left_live = own_cols >= 0
    targets = own_rows.reshape(row_total, col_groups, slot_total).transpose(1, 0, 2)

    def partial_blocks(left_blocks, gathered, wanted):
        safe_rows = jnp.clip(wanted, 0, blocks_total - 1)
        right_rows = gathered[safe_rows]
        right_cols = group_cols[safe_rows]
        matched = (
            (right_cols[:, :, :, None, :] == own_cols[None, :, None, :, None])
            & left_live[None, :, None, :, None]
            & (wanted >= 0)[:, :, :, None, None]
        )
        picked = jnp.where(
            matched[..., None, None],
            right_rows[:, :, :, None, :, :, :],
            jnp.zeros((), jnp.bfloat16),
        ).sum(axis=4)
        terms = jnp.einsum(
            "iapr,gisaqr->gispq", left_blocks, picked, preferred_element_type=jnp.float32
        )
        group_count = wanted.shape[0]
        return terms.reshape(group_count * row_total, slot_total, block_size, block_size)

    def product(left_blocks, right_blocks):
        gathered = lax.all_gather(right_blocks, "row", axis=0, tiled=True)
        return lax.psum_scatter(
            partial_blocks(left_blocks, gathered, targets), "col", scatter_dimension=0, tiled=True
        )

    scaled_step = product(step_dir, intersection).astype(jnp.bfloat16)
    change = (-(product(scaled_step, density) + product(density, scaled_step))).astype(jnp.bfloat16)
    commutator = (product(kohn_sham, change) - product(change, kohn_sham)).astype(jnp.bfloat16)
    local_trace = jnp.sum(change.astype(jnp.float32) * kohn_sham.astype(jnp.float32))
    trace_value = lax.psum(local_trace, ("row", "col")) / (blocks_total * block_size * block_size)
    return (commutator, trace_value)


def solution(mesh):
    in_specs = (
        P(),
        P("row", "col", None, None),
        P("row", "col", None, None),
        P("row", "col", None, None),
        P("row", "col", None, None),
    )
    out_specs = (P("row", "col", None, None), P())
    return jax.shard_map(
        per_device, mesh=mesh, in_specs=in_specs, out_specs=out_specs, check_vma=False
    )
```

profile of v0, /device:TPU:1, one launch (start us, length us, event | category | flops | bytes accessed | tf_op | source)
XLA Modules:
  0.0 501.8 jit_solution(6847474959793263105)
XLA Ops:
  9.5 0.8 broadcast_compare_fusion
  10.4 0.8 dynamic-slice_compare_fusion
  11.4 0.8 dynamic-slice_clamp_fusion
  14.0 50.7 %all-gather.14.cloned.1.call-done = bf16[64,2,128,128]{3,2,1,0:T(8,128)(2,1)} async-done(((bf16[4,2,128,128]{3,2,1,0:T(8,128)(2,1)}), bf16[64,2,128,128]{3,2,1,0:T(8,128)(2,1)}) %all-gather.14.cloned.1.call-update) | async-done | bytes 4194320 | tf_op jit(solution)/shard_map/all_gather | solution.py:42
  64.7 5.2 %gather_fusion.5 = bf16[64,2,128,128]{3,2,1,0:T(8,128)(2,1)} fusion(bf16[64,2,128,128]{3,2,1,0:T(8,128)(2,1)} %all-gather.14.cloned.1.call-done, s32[1024]{0:T(1024)S(1)} %pad_clamp_fusion), kind=kCustom, calls=%fused_computation.5 | custom fusion | bytes 8388864 | tf_op jit(solution)/shard_map/gather | solution.py:23
  69.9 48.0 %all-gather.8.cloned.1.call-done = bf16[64,2,128,128]{3,2,1,0:T(8,128)(2,1)} async-done(((bf16[4,2,128,128]{3,2,1,0:T(8,128)(2,1)}), bf16[64,2,128,128]{3,2,1,0:T(8,128)(2,1)}) %all-gather.8.cloned.1.call-update) | async-done | bytes 4194320 | tf_op jit(solution)/shard_map/all_gather | solution.py:42
  118.0 5.2 %gather_fusion.2 = bf16[64,2,128,128]{3,2,1,0:T(8,128)(2,1)} fusion(bf16[64,2,128,128]{3,2,1,0:T(8,128)(2,1)} %all-gather.8.cloned.1.call-done, s32[1024]{0:T(1024)S(1)} %pad_clamp_fusion), kind=kCustom, calls=%fused_computation.2 | custom fusion | bytes 8388864 | tf_op jit(solution)/shard_map/gather | solution.py:23
  123.2 48.1 %all-gather.6.cloned.1.call-done = bf16[64,2,128,128]{3,2,1,0:T(8,128)(2,1)} async-done(((bf16[4,2,128,128]{3,2,1,0:T(8,128)(2,1)}), bf16[64,2,128,128]{3,2,1,0:T(8,128)(2,1)}) %all-gather.6.cloned.1.call-update) | async-done | bytes 4194320 | tf_op jit(solution)/shard_map/all_gather | solution.py:42
  171.2 5.2 %gather_fusion.1 = bf16[64,2,128,128]{3,2,1,0:T(8,128)(2,1)} fusion(bf16[64,2,128,128]{3,2,1,0:T(8,128)(2,1)} %all-gather.6.cloned.1.call-done, s32[1024]{0:T(1024)S(1)} %pad_clamp_fusion), kind=kCustom, calls=%fused_computation.1 | custom fusion | bytes 8388864 | tf_op jit(solution)/shard_map/gather | solution.py:23
  176.5 17.5 %select_reduce_fusion = (bf16[8,4,2,2,128,128]{5,4,3,2,1,0:T(8,128)(2,1)}, bf16[8,4,2,2,128,128]{5,4,3,2,1,0:T(8,128)(2,1)S(1)}, bf16[8,4,2,2,128,128]{5,4,3,2,1,0:T(8,128)(2,1)}) fusion(pred[8,4,2,2,2]{4,3,2,1,0:T(4,128)(4,1)S(1)} %and_and_fusion, bf16[8,4,2,2,128,128]{5,4,3,2,1,0:T(8,128)(2,1)} %bitcast.70, bf16[8,4,2,2,128,128]{5,4,3,2,1,0:T(8,128)(2,1)} %bitcast.71, ...), kind=kLoop, calls=%fused_computation.6 | loop fusion | flops 18874368 | bytes 25166080 | tf_op jit(solution)/shard_map/reduce_sum | solution.py:34
  193.9 3.2 fusion.11
  197.1 5.4 %copy.48 = f32[8,4,2,128,128]{4,3,2,1,0:T(8,128)} copy(f32[8,4,2,128,128]{3,4,2,0,1:T(8,128)} %fusion.11) | data formatting | bytes 8388608 | tf_op jit(solution)/shard_map/iapr,gisaqr->gispq/transpose | solution.py:35
  202.6 34.9 %reduce-scatter.5.cloned.1.call-done = f32[4,2,128,128]{3,2,1,0:T(8,128)} async-done(((f32[32,2,128,128]{3,2,1,0:T(8,128)}), f32[4,2,128,128]{3,2,1,0:T(8,128)}) %reduce-scatter.5.cloned.1.call-update) | async-done | bytes 524304 | tf_op jit(solution)/shard_map/reduce_scatter | solution.py:43
  237.4 1.8 convert_element_type.10
  239.5 53.7 %all-gather.10.cloned.1.call-done = bf16[64,2,128,128]{3,2,1,0:T(8,128)(2,1)} async-done(((bf16[4,2,128,128]{3,2,1,0:T(8,128)(2,1)}), bf16[64,2,128,128]{3,2,1,0:T(8,128)(2,1)}) %all-gather.10.cloned.1.call-update) | async-done | bytes 4194320 | tf_op jit(solution)/shard_map/all_gather | solution.py:42
  293.2 5.2 %gather_fusion.3 = bf16[64,2,128,128]{3,2,1,0:T(8,128)(2,1)} fusion(bf16[64,2,128,128]{3,2,1,0:T(8,128)(2,1)} %all-gather.10.cloned.1.call-done, s32[1024]{0:T(1024)S(1)} %pad_clamp_fusion), kind=kCustom, calls=%fused_computation.3 | custom fusion | bytes 8388864 | tf_op jit(solution)/shard_map/gather | solution.py:23
  298.4 6.2 %select_reduce_fusion.2 = bf16[8,4,2,2,128,128]{5,4,3,2,1,0:T(8,128)(2,1)S(1)} fusion(pred[8,4,2,2,2]{4,3,2,1,0:T(4,128)(4,1)S(1)} %and_and_fusion, bf16[8,4,2,2,128,128]{5,4,3,2,1,0:T(8,128)(2,1)} %bitcast.69), kind=kLoop, calls=%fused_computation.8 | loop fusion | flops 6291456 | bytes 8388864 | tf_op jit(solution)/shard_map/reduce_sum | solution.py:34
  304.6 1.3 fusion.5
  305.9 0.9 copy-done.2
  306.8 3.2 fusion
  310.0 5.4 %copy.51 = f32[8,4,2,128,128]{4,3,2,1,0:T(8,128)} copy(f32[8,4,2,128,128]{3,4,2,0,1:T(8,128)} %fusion) | data formatting | bytes 8388608 | tf_op jit(solution)/shard_map/add | solution.py:48
  315.5 34.8 %reduce-scatter.11.cloned.1.call-done = f32[4,2,128,128]{3,2,1,0:T(8,128)} async-done(((f32[32,2,128,128]{3,2,1,0:T(8,128)}), f32[4,2,128,128]{3,2,1,0:T(8,128)}) %reduce-scatter.11.cloned.1.call-update) | async-done | bytes 524304 | tf_op jit(solution)/shard_map/reduce_scatter | solution.py:43
  350.3 2.4 multiply_reduce_fusion
  352.8 5.4 %fusion.17 = f32[8,4,2,128,128]{3,4,2,0,1:T(8,128)} fusion(bf16[8,4,2,2,128,128]{5,4,3,2,1,0:T(8,128)(2,1)} %get-tuple-element.2, bf16[4,2,128,128]{3,2,1,0:T(8,128)(2,1)} %get-tuple-element.6), kind=kOutput, calls=%fused_computation.25 | convolution fusion | flops 536870912 | bytes 8650752 | tf_op jit(solution)/shard_map/iapr,gisaqr->gispq/dot_general | solution.py:35
  358.2 5.4 %copy.55 = f32[8,4,2,128,128]{4,3,2,1,0:T(8,128)} copy(f32[8,4,2,128,128]{3,4,2,0,1:T(8,128)} %fusion.17) | data formatting | bytes 8388608 | tf_op jit(solution)/shard_map/iapr,gisaqr->gispq/transpose | solution.py:35
  363.6 42.6 %all-gather.12.cloned.1.call-done = bf16[64,2,128,128]{3,2,1,0:T(8,128)(2,1)} async-done(((bf16[4,2,128,128]{3,2,1,0:T(8,128)(2,1)}), bf16[64,2,128,128]{3,2,1,0:T(8,128)(2,1)}) %all-gather.12.cloned.1.call-update) | async-done | bytes 4194320 | tf_op jit(solution)/shard_map/all_gather | solution.py:42
  406.2 5.2 %gather_fusion.4 = bf16[64,2,128,128]{3,2,1,0:T(8,128)(2,1)} fusion(bf16[64,2,128,128]{3,2,1,0:T(8,128)(2,1)} %all-gather.12.cloned.1.call-done, s32[1024]{0:T(1024)S(1)} %pad_clamp_fusion), kind=kCustom, calls=%fused_computation.4 | custom fusion | bytes 8388864 | tf_op jit(solution)/shard_map/gather | solution.py:23
  411.5 6.2 %select_reduce_fusion.1 = bf16[8,4,2,2,128,128]{5,4,3,2,1,0:T(8,128)(2,1)S(1)} fusion(pred[8,4,2,2,2]{4,3,2,1,0:T(4,128)(4,1)S(1)} %and_and_fusion, bf16[8,4,2,2,128,128]{5,4,3,2,1,0:T(8,128)(2,1)} %bitcast.68), kind=kLoop, calls=%fused_computation.7 | loop fusion | flops 6291456 | bytes 8388864 | tf_op jit(solution)/shard_map/reduce_sum | solution.py:34
  417.6 3.2 fusion.14
  420.8 5.5 %copy.53 = f32[8,4,2,128,128]{4,3,2,1,0:T(8,128)} copy(f32[8,4,2,128,128]{3,4,2,0,1:T(8,128)} %fusion.14) | data formatting | bytes 8388608 | tf_op jit(solution)/shard_map/iapr,gisaqr->gispq/transpose | solution.py:35
  426.4 65.1 %psum.7 = f32[]{:T(128)} all-reduce(f32[]{:T(128)} %get-tuple-element.5), channel_id=1, replica_groups=mesh['row'=16,'col'=8] {'row','col'}, use_global_device_ids=true, to_apply=%region_11.12 | all-reduce | flops 1 | bytes 8 | tf_op jit(solution)/shard_map/psum | solution.py:51
  492.2 2.0 subtract_convert_fusion
  (44 shorter events, 5.0 us)
Async XLA Ops:
  7.2 186.8 %copy-start = (bf16[4,2,128,128]{3,2,1,0:T(8,128)(2,1)S(1)}, bf16[4,2,128,128]{3,2,1,0:T(8,128)(2,1)}, u32[]{:S(2)}) copy-start(bf16[4,2,128,128]{3,2,1,0:T(8,128)(2,1)} %param.6) | copy-start | bytes 786436
  7.2 57.5 %all-gather.14.cloned.1.call-start = ((), (), s32[]{:S(2)}) async-start(), calls=%async_computation.10 | async-start | bytes 4456448 | tf_op jit(solution)/shard_map/all_gather | solution.py:42
  7.9 110.1 %all-gather.8.cloned.1.call-start = ((), (), s32[]{:S(2)}) async-start(), calls=%async_computation.5 | async-start | bytes 4456448 | tf_op jit(solution)/shard_map/all_gather | solution.py:42
  8.7 162.6 %all-gather.6.cloned.1.call-start = ((), (), s32[]{:S(2)}) async-start(), calls=%async_computation.4 | async-start | bytes 4456448 | tf_op jit(solution)/shard_map/all_gather | solution.py:42
  9.4 228.0 %reduce-scatter.5.cloned.1.call-start = ((), (), s32[]{:S(2)}) async-start(), calls=%async_computation.6 | async-start | bytes 4718592 | tf_op jit(solution)/shard_map/reduce_scatter | solution.py:43
  202.5 90.7 %all-gather.10.cloned.1.call-start = ((), (), s32[]{:S(2)}) async-start(), calls=%async_computation.7 | async-start | bytes 4456448 | tf_op jit(solution)/shard_map/all_gather | solution.py:42
  239.2 111.0 %reduce-scatter.11.cloned.1.call-start = ((), (), s32[]{:S(2)}) async-start(), calls=%async_computation.12 | async-start | bytes 4718592 | tf_op jit(solution)/shard_map/reduce_scatter | solution.py:43
  298.4 6.2 %copy-start.4 = (bf16[4,2,128,128]{3,2,1,0:T(8,128)(2,1)S(1)}, bf16[4,2,128,128]{3,2,1,0:T(8,128)(2,1)}, u32[]{:S(2)}) copy-start(bf16[4,2,128,128]{3,2,1,0:T(8,128)(2,1)} %param.8) | copy-start | bytes 786436
  304.6 2.2 copy-start.2
  304.6 2.2 copy-start.3
  315.4 34.9 %copy-start.5 = (bf16[4,2,128,128]{3,2,1,0:T(8,128)(2,1)S(1)}, bf16[4,2,128,128]{3,2,1,0:T(8,128)(2,1)}, u32[]{:S(2)}) copy-start(bf16[4,2,128,128]{3,2,1,0:T(8,128)(2,1)} %param.9) | copy-start | bytes 786436
  315.4 90.8 %all-gather.12.cloned.1.call-start = ((), (), s32[]{:S(2)}) async-start(), calls=%async_computation.8 | async-start | bytes 4456448 | tf_op jit(solution)/shard_map/all_gather | solution.py:42
  352.7 139.4 %reduce-scatter.9.cloned.1.call-start = ((), (), s32[]{:S(2)}) async-start(), calls=%async_computation.11 | async-start | bytes 4718592 | tf_op jit(solution)/shard_map/reduce_scatter | solution.py:43
  363.6 128.6 %reduce-scatter.7.cloned.1.call-start = ((), (), s32[]{:S(2)}) async-start(), calls=%async_computation.9 | async-start | bytes 4718592 | tf_op jit(solution)/shard_map/reduce_scatter | solution.py:43
  420.8 73.3 %copy-start.1 = (bf16[4,2,128,128]{3,2,1,0:T(8,128)(2,1)S(1)}, bf16[4,2,128,128]{3,2,1,0:T(8,128)(2,1)}, u32[]{:S(2)}) copy-start(bf16[4,2,128,128]{3,2,1,0:T(8,128)(2,1)} %param.6) | copy-start | bytes 786436
Sparse Core Ops, SparseCore 0:
  10.1 54.5 all-gather.13
  66.8 51.0 all-gather.7
  120.1 51.0 all-gather.5
  202.6 34.7 reduce-scatter.4
  240.0 53.1 all-gather.9
  315.5 34.6 reduce-scatter.10
  353.0 53.2 all-gather.11
  408.6 35.0 reduce-scatter.8
  446.1 37.3 reduce-scatter.6
where the time goes:
time: 503 us; the launch traced here: 502 us
  waiting for transfers between devices  315 us (63%)
  blocking collectives  65.1 us (13%)
  local copies, waits for them, and re-layouts  50.7 us (10%)
  other arithmetic  38.5 us (8%)
  matrix products  16.3 us (3%)
  between operations  15.7 us (3%)
    all_gather x5, waiting for transfers between devices, product(): gathered = lax.all_gather(right_blocks, 'row', axis=0, tiled=True)  243 us
    reduce_scatter x4, waiting for transfers between devices, product(): lax.psum_scatter(partial_blocks(left_blocks, gathered, targets), 'col', s...  69.7 us
    psum x1, blocking collectives, per_device(): lax.psum(local_trace, ('row', 'col'))  65.1 us
    reduce_sum x3, other arithmetic, partial_blocks(): picked = jnp.where(matched[..., None, None], right_rows[:, :, :, None, :,...  29.8 us
    gather x5, local copies, waits for them, and re-layouts, partial_blocks(): right_rows = gathered[safe_rows]  26.1 us
    dot_general x5, matrix products, partial_blocks(): jnp.einsum('iapr,gisaqr->gispq', left_blocks, picked, preferred_element_t...  16.3 us
    transpose x3, local copies, waits for them, and re-layouts, partial_blocks(): jnp.einsum('iapr,gisaqr->gispq', left_blocks, picked, preferred_element_t...  16.2 us
  transfers between devices with their start and end apart: 9, of which 7 were waited for; matrix products, arithmetic and copies ran while one was open for 9% of the time, Pallas kernels for 0%

commit v1 on v0

--- a/solution.py
+++ b/solution.py
@@ -39,7 +39,9 @@
         return terms.reshape(group_count * row_total, slot_total, block_size, block_size)
 
     def product(left_blocks, right_blocks):
-        gathered = lax.all_gather(right_blocks, "row", axis=0, tiled=True)
+        gathered = jnp.concatenate(
+            lax.all_to_all(jnp.stack([right_blocks] * lax.axis_size("row")), "row", 0, 0), axis=0
+        )
         return lax.psum_scatter(
             partial_blocks(left_blocks, gathered, targets), "col", scatter_dimension=0, tiled=True
         )

time: 503 us -> 533 us (1.060)
  blocking collectives: 65.1 us -> 287 us
  waiting for transfers between devices: 315 us -> 114 us
  local copies, waits for them, and re-layouts: 50.7 us -> 58 us
    all_gather x5 -> x0, waiting for transfers between devices: 243 us -> none  [product(): gathered = lax.all_gather(right_blocks, 'row', axis=0, tiled=True)]
    all_to_all x0 -> x4, blocking collectives: none -> 217 us  [product(): lax.all_to_all(jnp.stack([right_blocks] * lax.axis_size('row')), 'row', 0...]
    all_to_all x0 -> x1, waiting for transfers between devices: none -> 36.6 us  [product(): lax.all_to_all(jnp.stack([right_blocks] * lax.axis_size('row')), 'row', 0...]
    another operation x0 -> x5, local copies, waits for them, and re-layouts: none -> 8.15 us  [product(): jnp.stack([right_blocks] * lax.axis_size('row'))]
    reduce_scatter x4, waiting for transfers between devices: 69.7 us -> 77.8 us  [product(): lax.psum_scatter(partial_blocks(left_blocks, gathered, targets), 'col', s...]
  transfers between devices with their start and end apart: 9 -> 5, of which waited for: 7 -> 3; matrix products, arithmetic and copies ran while one was open for 9% -> 6% of each run, Pallas kernels for 0% -> 0%
where the time goes in v1:
time: 533 us; the launch traced here: 532 us
  blocking collectives  287 us (54%)
  waiting for transfers between devices  114 us (21%)
  local copies, waits for them, and re-layouts  58 us (11%)
  other arithmetic  35 us (7%)
  matrix products  16.3 us (3%)
  between operations  15.7 us (3%)
    all_to_all x4, blocking collectives, product(): lax.all_to_all(jnp.stack([right_blocks] * lax.axis_size('row')), 'row', 0...  217 us
    reduce_scatter x4, waiting for transfers between devices, product(): lax.psum_scatter(partial_blocks(left_blocks, gathered, targets), 'col', s...  77.8 us
    psum x1, blocking collectives, per_device(): lax.psum(local_trace, ('row', 'col'))  70.1 us
    all_to_all x1, waiting for transfers between devices, product(): lax.all_to_all(jnp.stack([right_blocks] * lax.axis_size('row')), 'row', 0...  36.6 us
    reduce_sum x3, other arithmetic, partial_blocks(): picked = jnp.where(matched[..., None, None], right_rows[:, :, :, None, :,...  29.8 us
    gather x5, local copies, waits for them, and re-layouts, partial_blocks(): right_rows = gathered[safe_rows]  26.1 us
    dot_general x5, matrix products, partial_blocks(): jnp.einsum('iapr,gisaqr->gispq', left_blocks, picked, preferred_element_t...  16.3 us
    transpose x3, local copies, waits for them, and re-layouts, partial_blocks(): jnp.einsum('iapr,gisaqr->gispq', left_blocks, picked, preferred_element_t...  16.1 us
  transfers between devices with their start and end apart: 5, of which 3 were waited for; matrix products, arithmetic and copies ran while one was open for 6% of the time, Pallas kernels for 0%

profile of v1, /device:TPU:1, one launch (start us, length us, event | category | flops | bytes accessed | tf_op | source)
XLA Modules:
  0.0 531.6 jit_solution(13677061195934914535)
XLA Ops:
  7.2 2.0 stack.11
  9.2 57.9 %all_to_all.25 = bf16[16,4,2,128,128]{4,3,2,1,0:T(8,128)(2,1)} all-to-all(bf16[16,4,2,128,128]{4,3,2,1,0:T(8,128)(2,1)S(1)} %stack.11), channel_id=1, replica_groups=mesh['row'=16,'col'=8] {'row'}, dimensions={0} | all-to-all | bytes 8388608 | tf_op jit(solution)/shard_map/all_to_all | solution.py:43
  67.1 1.0 stack.10
  68.2 53.3 %all_to_all.26 = bf16[16,4,2,128,128]{4,3,2,1,0:T(8,128)(2,1)} all-to-all(bf16[16,4,2,128,128]{4,3,2,1,0:T(8,128)(2,1)S(1)} %stack.10), channel_id=1, replica_groups=mesh['row'=16,'col'=8] {'row'}, dimensions={0} | all-to-all | bytes 8388608 | tf_op jit(solution)/shard_map/all_to_all | solution.py:43
  121.5 3.0 stack.14
  124.5 4.7 all-to-all-start.4
  131.2 5.2 gather_fusion.2
  136.4 5.2 gather_fusion.1
  141.7 36.6 %all-to-all-done.4 = bf16[16,4,2,128,128]{4,3,2,1,0:T(8,128)(2,1)} async-done(((bf16[16,4,2,128,128]{4,3,2,1,0:T(8,128)(2,1)}), bf16[16,4,2,128,128]{4,3,2,1,0:T(8,128)(2,1)}, u32[]{:S(2)}, u32[]{:S(2)}) %all-to-all-start.4) | async-done | bytes 4194336 | tf_op jit(solution)/shard_map/all_to_all | solution.py:43
  178.2 5.2 gather_fusion.5
  183.4 17.5 %select_reduce_fusion = (bf16[8,4,2,2,128,128]{5,4,3,2,1,0:T(8,128)(2,1)}, bf16[8,4,2,2,128,128]{5,4,3,2,1,0:T(8,128)(2,1)S(1)}, bf16[8,4,2,2,128,128]{5,4,3,2,1,0:T(8,128)(2,1)}) fusion(pred[8,4,2,2,2]{4,3,2,1,0:T(4,128)(4,1)S(1)} %and_and_fusion, bf16[8,4,2,2,128,128]{5,4,3,2,1,0:T(8,128)(2,1)} %bitcast.81, bf16[8,4,2,2,128,128]{5,4,3,2,1,0:T(8,128)(2,1)} %bitcast.79, ...), kind=kLoop, calls=%fused_computation.6 | loop fusion | flops 18874368 | bytes 25166080 | tf_op jit(solution)/shard_map/reduce_sum | solution.py:34
  200.9 3.2 fusion.11
  204.1 5.3 %copy.36 = f32[8,4,2,128,128]{4,3,2,1,0:T(8,128)} copy(f32[8,4,2,128,128]{3,4,2,0,1:T(8,128)} %fusion.11) | data formatting | bytes 8388608 | tf_op jit(solution)/shard_map/iapr,gisaqr->gispq/transpose | solution.py:35
  209.6 39.8 %reduce-scatter.5.cloned.1.call-done = f32[4,2,128,128]{3,2,1,0:T(8,128)} async-done(((f32[32,2,128,128]{3,2,1,0:T(8,128)}), f32[4,2,128,128]{3,2,1,0:T(8,128)}) %reduce-scatter.5.cloned.1.call-update) | async-done | bytes 524304 | tf_op jit(solution)/shard_map/reduce_scatter | solution.py:45
  249.4 1.1 convert_element_type.10
  251.5 52.9 %all_to_all.27 = bf16[16,4,2,128,128]{4,3,2,1,0:T(8,128)(2,1)} all-to-all(bf16[16,4,2,128,128]{4,3,2,1,0:T(8,128)(2,1)S(1)} %stack.12), channel_id=1, replica_groups=mesh['row'=16,'col'=8] {'row'}, dimensions={0} | all-to-all | bytes 8388608 | tf_op jit(solution)/shard_map/all_to_all | solution.py:43
  304.4 5.2 gather_fusion.3
  309.7 6.2 %select_reduce_fusion.2 = bf16[8,4,2,2,128,128]{5,4,3,2,1,0:T(8,128)(2,1)S(1)} fusion(pred[8,4,2,2,2]{4,3,2,1,0:T(4,128)(4,1)S(1)} %and_and_fusion, bf16[8,4,2,2,128,128]{5,4,3,2,1,0:T(8,128)(2,1)} %bitcast.78), kind=kLoop, calls=%fused_computation.8 | loop fusion | flops 6291456 | bytes 8388864 | tf_op jit(solution)/shard_map/reduce_sum | solution.py:34
  315.8 1.3 fusion.5
  318.0 3.2 fusion
  321.2 5.3 %copy.39 = f32[8,4,2,128,128]{4,3,2,1,0:T(8,128)} copy(f32[8,4,2,128,128]{3,4,2,0,1:T(8,128)} %fusion) | data formatting | bytes 8388608 | tf_op jit(solution)/shard_map/add | solution.py:50
  326.7 37.9 %reduce-scatter.11.cloned.1.call-done = f32[4,2,128,128]{3,2,1,0:T(8,128)} async-done(((f32[32,2,128,128]{3,2,1,0:T(8,128)}), f32[4,2,128,128]{3,2,1,0:T(8,128)}) %reduce-scatter.11.cloned.1.call-update) | async-done | bytes 524304 | tf_op jit(solution)/shard_map/reduce_scatter | solution.py:45
  364.6 1.8 multiply_reduce_fusion
  366.3 5.4 %fusion.17 = f32[8,4,2,128,128]{3,4,2,0,1:T(8,128)} fusion(bf16[8,4,2,2,128,128]{5,4,3,2,1,0:T(8,128)(2,1)} %get-tuple-element.2, bf16[4,2,128,128]{3,2,1,0:T(8,128)(2,1)S(1)} %get-tuple-element.6), kind=kOutput, calls=%fused_computation.25 | convolution fusion | flops 536870912 | bytes 8650752 | tf_op jit(solution)/shard_map/iapr,gisaqr->gispq/dot_general | solution.py:35
  371.8 5.4 %copy.43 = f32[8,4,2,128,128]{4,3,2,1,0:T(8,128)} copy(f32[8,4,2,128,128]{3,4,2,0,1:T(8,128)} %fusion.17) | data formatting | bytes 8388608 | tf_op jit(solution)/shard_map/iapr,gisaqr->gispq/transpose | solution.py:35
  378.2 53.0 %all_to_all.28 = bf16[16,4,2,128,128]{4,3,2,1,0:T(8,128)(2,1)} all-to-all(bf16[16,4,2,128,128]{4,3,2,1,0:T(8,128)(2,1)S(1)} %stack.13), channel_id=1, replica_groups=mesh['row'=16,'col'=8] {'row'}, dimensions={0} | all-to-all | bytes 8388608 | tf_op jit(solution)/shard_map/all_to_all | solution.py:43
  431.2 5.2 gather_fusion.4
  436.4 6.2 %select_reduce_fusion.1 = bf16[8,4,2,2,128,128]{5,4,3,2,1,0:T(8,128)(2,1)S(1)} fusion(pred[8,4,2,2,2]{4,3,2,1,0:T(4,128)(4,1)S(1)} %and_and_fusion, bf16[8,4,2,2,128,128]{5,4,3,2,1,0:T(8,128)(2,1)} %bitcast.75), kind=kLoop, calls=%fused_computation.7 | loop fusion | flops 6291456 | bytes 8388864 | tf_op jit(solution)/shard_map/reduce_sum | solution.py:34
  442.6 3.2 fusion.14
  445.8 5.4 %copy.41 = f32[8,4,2,128,128]{4,3,2,1,0:T(8,128)} copy(f32[8,4,2,128,128]{3,4,2,0,1:T(8,128)} %fusion.14) | data formatting | bytes 8388608 | tf_op jit(solution)/shard_map/iapr,gisaqr->gispq/transpose | solution.py:35
  451.3 70.1 %psum.7 = f32[]{:T(128)} all-reduce(f32[]{:T(128)} %get-tuple-element.5), channel_id=1, replica_groups=mesh['row'=16,'col'=8] {'row','col'}, use_global_device_ids=true, to_apply=%region_11.12 | all-reduce | flops 1 | bytes 8 | tf_op jit(solution)/shard_map/psum | solution.py:53
  522.0 2.0 subtract_convert_fusion
  (40 shorter events, 5.2 us)
Async XLA Ops:
  7.2 193.8 %copy-start = (bf16[4,2,128,128]{3,2,1,0:T(8,128)(2,1)S(1)}, bf16[4,2,128,128]{3,2,1,0:T(8,128)(2,1)}, u32[]{:S(2)}) copy-start(bf16[4,2,128,128]{3,2,1,0:T(8,128)(2,1)} %param.6) | copy-start | bytes 786436
  9.2 57.9 %copy-start.3 = (bf16[4,2,128,128]{3,2,1,0:T(8,128)(2,1)S(1)}, bf16[4,2,128,128]{3,2,1,0:T(8,128)(2,1)}, u32[]{:S(2)}) copy-start(bf16[4,2,128,128]{3,2,1,0:T(8,128)(2,1)} %param.8) | copy-start | bytes 786436
  68.2 53.3 %copy-start.4 = (bf16[4,2,128,128]{3,2,1,0:T(8,128)(2,1)S(1)}, bf16[4,2,128,128]{3,2,1,0:T(8,128)(2,1)}, u32[]{:S(2)}) copy-start(bf16[4,2,128,128]{3,2,1,0:T(8,128)(2,1)} %param.9) | copy-start | bytes 786436
  124.5 4.9 copy-start.5
  124.5 53.8 %all-to-all-start.4 = ((bf16[16,4,2,128,128]{4,3,2,1,0:T(8,128)(2,1)}), bf16[16,4,2,128,128]{4,3,2,1,0:T(8,128)(2,1)}, u32[]{:S(2)}, u32[]{:S(2)}) async-start(bf16[16,4,2,128,128]{4,3,2,1,0:T(8,128)(2,1)} %stack.14), calls=%async_computation.6 | async-start | bytes 8388608 | tf_op jit(solution)/shard_map/all_to_all | solution.py:43
  129.2 120.2 %reduce-scatter.5.cloned.1.call-start = ((), (), s32[]{:S(2)}) async-start(), calls=%async_computation.9 | async-start | bytes 4718592 | tf_op jit(solution)/shard_map/reduce_scatter | solution.py:45
  209.5 155.0 %reduce-scatter.11.cloned.1.call-start = ((), (), s32[]{:S(2)}) async-start(), calls=%async_computation.12 | async-start | bytes 4718592 | tf_op jit(solution)/shard_map/reduce_scatter | solution.py:45
  315.8 2.2 copy-start.2
  326.6 195.4 %reduce-scatter.9.cloned.1.call-start = ((), (), s32[]{:S(2)}) async-start(), calls=%async_computation.11 | async-start | bytes 4718592 | tf_op jit(solution)/shard_map/reduce_scatter | solution.py:45
  377.1 144.9 %reduce-scatter.7.cloned.1.call-start = ((), (), s32[]{:S(2)}) async-start(), calls=%async_computation.10 | async-start | bytes 4718592 | tf_op jit(solution)/shard_map/reduce_scatter | solution.py:45
  445.8 78.1 %copy-start.1 = (bf16[4,2,128,128]{3,2,1,0:T(8,128)(2,1)S(1)}, bf16[4,2,128,128]{3,2,1,0:T(8,128)(2,1)}, u32[]{:S(2)}) copy-start(bf16[4,2,128,128]{3,2,1,0:T(8,128)(2,1)} %param.6) | copy-start | bytes 786436
Sparse Core Ops, SparseCore 0:
  209.6 39.7 reduce-scatter.4
  326.7 37.7 reduce-scatter.10
  377.3 37.4 reduce-scatter.8
  451.4 38.3 reduce-scatter.6
